TPU v7x, 32 devices: a whole 2x2x4 slice. The times are simulated.
32 devices in a mesh: view: 4 (over y, core), bx: 2 (over x), by: 4 (over z).
Axes of the slice: x: 2, y: 2, z: 4, core: 2. Of those that a mesh axis runs over, the one named last changes fastest.
Arguments:
- estimate: float32 [2048, 512], P(('bx', 'by')), may hold values from 0.5 to 2
- recorded: float32 [4, 2048, 512], P('view', ('bx', 'by')), may hold values from 0.5 to 4
- resample: float32 [4, 4, 512, 512], P('view'), may hold values from 0 to 1, as said below
- psf_taps: float32 [4, 31], P('view'), may hold values from 0.2 to 1
- source_brick: int32 [4, 2048, 4], P('view', ('bx', 'by')), may hold values from 0 to 7, all different within a row; in each aligned block of 256 rows (0 to 255, 256 to 511, ..., all dimensions but the last counted through in order) at most 192 rows name the same one
- source_column: int32 [4, 2048, 4], P('view', ('bx', 'by')), may hold values from 0 to 255
Outputs:
- refined: float32 [2048, 512], P(('bx', 'by'))
Inputs may be any that keep to these rules, and one draw needn't show every extreme that they name: `source_brick`: in each view, the 4 bricks named for one column are different; among the columns of one brick, no joined brick is named more than 192 times, and some joined brick exactly 192 times. `resample`: all entries are nonnegative.
All inputs are finite; a program needn't handle non-finite values.
Results may differ from a plain program's by a relative error of at most 0.0001.
Values sent between devices are 32-bit elements; how exact they have to be, the bound alone decides.
A program may use at most 192 MiB of HBM per device.

v0:
```python
import jax
import jax.numpy as jnp
from jax import lax
from jax.sharding import PartitionSpec as P

ITERS = 2
precise = lax.Precision.HIGHEST


def blur_matrix(taps_row, column_len):
    spread = taps_row / jnp.sum(taps_row)
    tap_count = spread.shape[0]
    half_width = (tap_count - 1) // 2
    row_ids = lax.broadcasted_iota(jnp.int32, (column_len, column_len), 0)
    col_ids = lax.broadcasted_iota(jnp.int32, (column_len, column_len), 1)
    offset = row_ids - col_ids + half_width
    matrix = jnp.zeros((column_len, column_len), jnp.float32)
    for tap_number in range(tap_count):
        matrix = matrix + jnp.where(offset == tap_number, spread[tap_number], 0.0)
    return matrix


def per_device(estimate, recorded, resample, psf_taps, source_brick, source_column):
    bricks_x = lax.axis_size("bx")
    bricks_y = lax.axis_size("by")
    peer_count = bricks_x * bricks_y
    columns, column_len = estimate.shape
    sources = source_brick.shape[2]
    pair_count = columns * sources
    capacity = 3 * pair_count // (2 * peer_count)
    peer_ids = source_brick[0].reshape(pair_count)
    wanted = source_column[0].reshape(pair_count)
    branch_ids = lax.broadcasted_iota(jnp.int32, (columns, sources), 1).reshape(pair_count)
    peer_hits = (
        peer_ids[:, None] == lax.broadcasted_iota(jnp.int32, (pair_count, peer_count), 1)
    ).astype(jnp.int32)
    before = jnp.cumsum(peer_hits, axis=0) - peer_hits
    slot_rank = jnp.sum(before * peer_hits, axis=1)
    position = peer_ids * capacity + slot_rank
    request = (
        jnp.full((peer_count * capacity,), -1, jnp.int32)
        .at[position]
        .set(wanted * sources + branch_ids)
    )
    served = lax.all_to_all(
        request.reshape(peer_count, capacity), ("bx", "by"), split_axis=0, concat_axis=0, tiled=True
    )
    served = served.reshape(peer_count * capacity)
    owned_column = jnp.maximum(served, 0) // sources
    weights = resample[0]
    blurring = blur_matrix(psf_taps[0], column_len)
    unit_smeared = jnp.sum(blurring, axis=1)
    unit_back = jnp.einsum("b,kcb->kc", unit_smeared, weights, precision=precise)
    normalizer = None
    norm_local = None
    for sweep in range(ITERS):
        outgoing = estimate[owned_column]
        incoming = lax.all_to_all(
            outgoing.reshape(peer_count, capacity, column_len),
            ("bx", "by"),
            split_axis=0,
            concat_axis=0,
            tiled=True,
        )
        incoming = incoming.reshape(peer_count * capacity, column_len)
        pieces = incoming[position].reshape(columns, sources, column_len)
        forward = jnp.einsum("qkb,kbc->qc", pieces, weights, precision=precise)
        blurred = jnp.dot(forward, blurring, precision=precise)
        quotient = recorded[0] / blurred
        smeared = jnp.dot(quotient, blurring.T, precision=precise)
        contributions = jnp.einsum("qb,kcb->qkc", smeared, weights, precision=precise).reshape(
            pair_count, column_len
        )
        with_units = sweep == 0
        if with_units:
            unit_rows = jnp.broadcast_to(unit_back[None], (columns, sources, column_len)).reshape(
                pair_count, column_len
            )
            stacked = jnp.stack([contributions, unit_rows], axis=1)
        else:
            stacked = contributions[:, None, :]
        layers = stacked.shape[1]
        buffer = (
            jnp.zeros((peer_count * capacity, layers, column_len), jnp.float32)
            .at[position]
            .set(stacked)
        )
        returned = lax.all_to_all(
            buffer.reshape(peer_count, capacity, layers, column_len),
            ("bx", "by"),
            split_axis=0,
            concat_axis=0,
            tiled=True,
        )
        returned = returned.reshape(peer_count * capacity, layers, column_len)
        owned_sum = (
            jnp.zeros((columns, layers, column_len), jnp.float32).at[owned_column].add(returned)
        )
        correction_local = owned_sum[:, 0]
        if with_units:
            norm_local = owned_sum[:, 1]
        if sweep == 0:
            summands = jnp.stack([correction_local, norm_local])
        else:
            summands = correction_local[None]
        view_total = lax.psum(summands, "view")
        if sweep == 0:
            normalizer = view_total[1]
        estimate = estimate * (view_total[0] + 1.0) / (normalizer + 1.0)
    return estimate


def solution(mesh):
    return jax.shard_map(
        per_device,
        mesh=mesh,
        in_specs=(
            P(("bx", "by"), None),
            P("view", ("bx", "by"), None),
            P("view", None, None, None),
            P("view", None),
            P("view", ("bx", "by"), None),
            P("view", ("bx", "by"), None),
        ),
        out_specs=P(("bx", "by"), None),
        check_vma=False,
    )
```

profile of v0, /device:TPU:0, one launch (start us, length us, event | category | flops | bytes accessed | tf_op | source)
XLA Modules:
  0.0 890.5 jit_solution(9087115394177621034)
XLA Ops:
  8.4 2.3 reduce-window.6
  12.6 4.3 scatter_custom_fusion
  17.0 13.6 %all_to_all.29 = s32[8,1,192]{2,1,0:T(1,128)S(1)} all-to-all(s32[8,1,192]{2,1,0:T(1,128)S(1)} %all_to_all.18), channel_id=1, replica_groups=mesh['view'=4,'bx'=2,'by'=4] {'bx','by'}, dimensions={0} | all-to-all | bytes 12288 | tf_op jit(solution)/shard_map/all_to_all | solution.py:45
  30.8 5.0 gather_fusion
  35.7 4.6 all-to-all-start.1
  43.2 22.8 %fusion.58 = f32[512]{0:T(512)S(1)} fusion(f32[]{:T(128)} %bitcast.38, f32[]{:T(128)} %bitcast.37, f32[]{:T(128)} %bitcast.36, f32[]{:T(128)} %bitcast.35, f32[]{:T(128)} %bitcast.34, f32[]{:T(128)} %bitcast.33, f32[]{:T(128)} %bitcast.32, f32[]{:T(128)} %bitcast.31, f32[]{:T(128)} %bitcast.30, f32[]{:T(128)} %bitcast.29, f32[]{:T(128)} %bitcast.28, ...), kind=kLoop, calls=%fused_computation.73 | loop fusion | flops 24903168 | bytes 2172 | tf_op jit(solution)/shard_map/reduce_sum | solution.py:52
  66.0 5.7 fusion.4
  73.7 37.0 %all-to-all-done.1 = f32[8,192,512]{2,1,0:T(8,128)} async-done(((f32[8,192,512]{2,1,0:T(8,128)}), f32[8,192,512]{2,1,0:T(8,128)}, u32[]{:S(2)}, u32[]{:S(2)}) %all-to-all-start.1) | async-done | bytes 3145760 | tf_op jit(solution)/shard_map/all_to_all | solution.py:58
  110.7 5.9 gather_fusion.1
  118.3 7.2 fusion.14
  125.6 24.4 %convolution_divide_fusion.1 = f32[256,512]{1,0:T(8,128)S(1)} fusion(f32[256,512]{1,0:T(8,128)S(1)} %fusion.14, f32[1,256,512]{2,1,0:T(8,128)S(1)} %copy-done.5, f32[]{:T(128)} %bitcast.38, f32[]{:T(128)} %bitcast.37, f32[]{:T(128)} %bitcast.36, f32[]{:T(128)} %bitcast.35, f32[]{:T(128)} %bitcast.34, f32[]{:T(128)} %bitcast.33, f32[]{:T(128)} %bitcast.32, ...), kind=kOutput, calls=%fused_computation.25 | convolution fusion | flops 830078976 | bytes 1572988 | tf_op jit(solution)/shard_map/dot_general | solution.py:68
  150.0 25.1 %convolution_bitcast_fusion.1 = f32[256,512,1]{1,0,2:T(8,128)S(1)} fusion(f32[256,512]{1,0:T(8,128)S(1)} %convolution_divide_fusion.1, f32[]{:T(128)} %bitcast.38, f32[]{:T(128)} %bitcast.37, f32[]{:T(128)} %bitcast.36, f32[]{:T(128)} %bitcast.35, f32[]{:T(128)} %bitcast.34, f32[]{:T(128)} %bitcast.33, f32[]{:T(128)} %bitcast.32, f32[]{:T(128)} %bitcast.31, ...), kind=kOutput, calls=%fused_computation.29 | convolution fusion | flops 829947904 | bytes 1048700 | tf_op jit(solution)/shard_map/dot_general | solution.py:70
  175.1 3.7 fusion.6
  182.0 2.7 pad_maximum_fusion
  184.6 5.3 copy.45
  189.9 4.3 broadcast_in_dim.160
  194.2 104.3 %scatter_fusion = f32[1536,2,512]{2,1,0:T(2,128)} fusion(f32[1536,2,512]{2,1,0:T(2,128)} %broadcast_in_dim.160, s32[1024]{0:T(1024)S(1)} %bitcast.129, f32[1024,2,512]{2,1,0:T(2,128)} %copy.45), kind=kCustom, calls=%fused_computation.5 | custom fusion | bytes 12587008 | tf_op jit(solution)/shard_map/scatter | solution.py:86
  298.5 142.2 %all_to_all.30 = f32[8,192,2,512]{3,2,1,0:T(2,128)} all-to-all(f32[8,192,2,512]{3,2,1,0:T(2,128)} %bitcast.120), channel_id=1, replica_groups=mesh['view'=4,'bx'=2,'by'=4] {'bx','by'}, dimensions={0} | all-to-all | bytes 12582912 | tf_op jit(solution)/shard_map/all_to_all | solution.py:88
  441.0 122.5 %scatter_fusion.1 = f32[256,2,512]{2,1,0:T(2,128)S(1)} fusion(f32[256,2,512]{2,1,0:T(2,128)S(1)} %broadcast_in_dim.158, s32[1536]{0:T(1024)S(1)} %fusion.67, f32[1536,2,512]{2,1,0:T(2,128)} %bitcast.121), kind=kCustom, calls=%fused_computation.6 | custom fusion | flops 1572864 | bytes 18880512 | tf_op jit(solution)/shard_map/scatter-add | solution.py:97
  566.4 34.1 %all-reduce.3.cloned.1.call-done = f32[2,256,512]{2,0,1:T(2,128)} async-done(((f32[2,256,512]{2,0,1:T(2,128)}), f32[2,256,512]{2,0,1:T(2,128)}) %all-reduce.3.cloned.1.call-update) | async-done | bytes 1048592 | tf_op jit(solution)/shard_map/psum | solution.py:106
  600.5 2.6 slice_add_fusion
  604.1 5.0 gather_fusion.2
  609.0 76.9 %all_to_all.31 = f32[8,192,512]{2,1,0:T(8,128)} all-to-all(f32[8,192,512]{2,1,0:T(8,128)} %bitcast.124), channel_id=1, replica_groups=mesh['view'=4,'bx'=2,'by'=4] {'bx','by'}, dimensions={0} | all-to-all | bytes 6291456 | tf_op jit(solution)/shard_map/all_to_all | solution.py:58
  685.9 5.9 gather_fusion.3
  693.5 7.2 fusion.19
  700.7 24.4 %convolution_divide_fusion = f32[256,512]{1,0:T(8,128)S(1)} fusion(f32[256,512]{1,0:T(8,128)S(1)} %fusion.19, f32[1,256,512]{2,1,0:T(8,128)S(1)} %copy-done.6, f32[]{:T(128)} %bitcast.38, f32[]{:T(128)} %bitcast.37, f32[]{:T(128)} %bitcast.36, f32[]{:T(128)} %bitcast.35, f32[]{:T(128)} %bitcast.34, f32[]{:T(128)} %bitcast.33, f32[]{:T(128)} %bitcast.32, ...), kind=kOutput, calls=%fused_computation.24 | convolution fusion | flops 830078976 | bytes 1572988 | tf_op jit(solution)/shard_map/dot_general | solution.py:68
  725.2 24.9 %convolution_bitcast_fusion = f32[256,512,1]{1,0,2:T(8,128)S(1)} fusion(f32[256,512]{1,0:T(8,128)S(1)} %convolution_divide_fusion, f32[]{:T(128)} %bitcast.38, f32[]{:T(128)} %bitcast.37, f32[]{:T(128)} %bitcast.36, f32[]{:T(128)} %bitcast.35, f32[]{:T(128)} %bitcast.34, f32[]{:T(128)} %bitcast.33, f32[]{:T(128)} %bitcast.32, f32[]{:T(128)} %bitcast.31, ...), kind=kOutput, calls=%fused_computation.28 | convolution fusion | flops 829947904 | bytes 1048700 | tf_op jit(solution)/shard_map/dot_general | solution.py:70
  750.1 3.7 fusion
  756.9 7.3 scatter_custom_fusion.3
  764.2 74.6 %all_to_all.32 = f32[8,192,1,512]{3,1,2,0:T(8,128)} all-to-all(f32[8,192,1,512]{3,1,2,0:T(8,128)} %bitcast.122), channel_id=1, replica_groups=mesh['view'=4,'bx'=2,'by'=4] {'bx','by'}, dimensions={0} | all-to-all | bytes 6291456 | tf_op jit(solution)/shard_map/all_to_all | solution.py:88
  838.8 11.5 %scatter_custom_fusion.4 = f32[256,512]{1,0:T(8,128)} fusion(s32[1536]{0:T(1024)S(1)} %fusion.67, f32[1536,512]{1,0:T(8,128)} %bitcast.125, f32[]{:T(128)} %constant.37.clone.1), kind=kCustom, calls=%fused_computation.74 | custom fusion | flops 786432 | bytes 524800 | tf_op jit(solution)/shard_map/scatter-add | solution.py:97
  850.3 31.2 %all-reduce.5.cloned.1.call-done = f32[1,256,512]{2,1,0:T(8,128)} async-done(((f32[1,256,512]{2,1,0:T(8,128)}), f32[1,256,512]{2,1,0:T(8,128)}) %all-reduce.5.cloned.1.call-update) | async-done | bytes 524304 | tf_op jit(solution)/shard_map/psum | solution.py:106
  (64 shorter events, 24.6 us)
Async XLA Ops:
  6.5 24.2 %copy-start = (f32[256,512]{1,0:T(8,128)S(1)}, f32[256,512]{1,0:T(8,128)}, u32[]{:S(2)}) copy-start(f32[256,512]{1,0:T(8,128)} %param.6) | copy-start | bytes 1572868
  35.7 4.8 copy-start.7
  35.7 75.0 %all-to-all-start.1 = ((f32[8,192,512]{2,1,0:T(8,128)}), f32[8,192,512]{2,1,0:T(8,128)}, u32[]{:S(2)}, u32[]{:S(2)}) async-start(f32[8,192,512]{2,1,0:T(8,128)} %bitcast.123), calls=%async_computation.1 | async-start | bytes 6291456 | tf_op jit(solution)/shard_map/all_to_all | solution.py:58
  40.3 560.2 %all-reduce.3.cloned.1.call-start = ((), (), s32[]{:S(2)}) async-start(), calls=%async_computation.5 | async-start | bytes 2097152 | tf_op jit(solution)/shard_map/psum | solution.py:106
  118.3 7.2 copy-start.5
  150.0 25.1 %copy-start.1 = (f32[1,4,512,512]{3,2,1,0:T(8,128)S(1)}, f32[1,4,512,512]{3,2,1,0:T(8,128)}, u32[]{:S(2)}) copy-start(f32[1,4,512,512]{3,2,1,0:T(8,128)} %param.8) | copy-start | bytes 12582916
  566.3 315.1 %all-reduce.5.cloned.1.call-start = ((), (), s32[]{:S(2)}) async-start(), calls=%async_computation.6 | async-start | bytes 1048576 | tf_op jit(solution)/shard_map/psum | solution.py:106
  603.1 0.8 copy-start.3
  693.5 7.2 copy-start.6
  725.2 24.9 %copy-start.2 = (f32[1,4,512,512]{3,2,1,0:T(8,128)S(1)}, f32[1,4,512,512]{3,2,1,0:T(8,128)}, u32[]{:S(2)}) copy-start(f32[1,4,512,512]{3,2,1,0:T(8,128)} %param.8) | copy-start | bytes 12582916
  764.2 117.3 %copy-start.4 = (f32[1,256,512]{2,0,1:T(1,128)S(1)}, f32[1,256,512]{2,0,1:T(1,128)}, u32[]{:S(2)}) copy-start(f32[1,256,512]{2,0,1:T(1,128)} %copy-done.3) | copy-start | bytes 1572868
Sparse Core Ops, SparseCore 0:
  566.4 34.0 all-reduce.2
  850.4 30.9 all-reduce.4
where the time goes:
time: 903 us; the launch traced here: 891 us
  blocking collectives  307 us (34%)
  other arithmetic  171 us (19%)
  local copies, waits for them, and re-layouts  164 us (18%)
  matrix products  126 us (14%)
  waiting for transfers between devices  102 us (11%)
  between operations  14 us (2%)
    all_to_all x2, blocking collectives, per_device(): lax.all_to_all(buffer.reshape(peer_count, capacity, layers, column_len),...  217 us
    scatter-add x2, other arithmetic, per_device(): jnp.zeros((columns, layers, column_len), jnp.float32).at[owned_column]  134 us
    scatter x2, local copies, waits for them, and re-layouts, per_device(): buffer = jnp.zeros((peer_count * capacity, layers, column_len), jnp.float...  112 us
    all_to_all x1, blocking collectives, per_device(): lax.all_to_all(outgoing.reshape(peer_count, capacity, column_len), ('bx',...  76.9 us
    psum x2, waiting for transfers between devices, per_device(): view_total = lax.psum(summands, 'view')  65.3 us
    dot_general x2, matrix products, per_device(): smeared = jnp.dot(quotient, blurring.T, precision=precise)  49.9 us
    dot_general x2, matrix products, per_device(): blurred = jnp.dot(forward, blurring, precision=precise)  48.8 us
    all_to_all x1, waiting for transfers between devices, per_device(): lax.all_to_all(outgoing.reshape(peer_count, capacity, column_len), ('bx',...  37 us
  transfers between devices with their start and end apart: 3, of which 3 were waited for; matrix products, arithmetic and copies ran while one was open for 4% of the time, Pallas kernels for 0%

commit v1 on v0

--- a/solution.py
+++ b/solution.py
@@ -1,3 +1,4 @@
+import functools
 import jax
 import jax.numpy as jnp
 from jax import lax
@@ -5,6 +6,19 @@
 
 ITERS = 2
 precise = lax.Precision.HIGHEST
+
+
+def thing_raise(xin, chip_axis):
+    n_peers_all = jax.lax.axis_size(chip_axis)
+    f_next = xin
+    for q in [
+        [(dev, dev ^ k) for dev in range(n_peers_all)] for k in (1, 2, 4, 8, 16) if k < n_peers_all
+    ]:
+        f_next = f_next + jax.lax.ppermute(f_next, chip_axis, q)
+    return f_next
+
+
+register_the_stacks_all = functools.partial(thing_raise, chip_axis="view")
 
 
 def blur_matrix(taps_row, column_len):
@@ -103,7 +117,7 @@
             summands = jnp.stack([correction_local, norm_local])
         else:
             summands = correction_local[None]
-        view_total = lax.psum(summands, "view")
+        view_total = register_the_stacks_all(summands)
         if sweep == 0:
             normalizer = view_total[1]
         estimate = estimate * (view_total[0] + 1.0) / (normalizer + 1.0)

time: 903 us -> 866 us (0.959)
  waiting for transfers between devices: 102 us -> 77.6 us
  between operations: 14 us -> 0.56 us
    psum x2 -> x0, waiting for transfers between devices: 65.3 us -> none  [per_device(): view_total = lax.psum(summands, 'view')]
    ppermute x0 -> x4, waiting for transfers between devices: none -> 40.3 us  [thing_raise(): f_next = f_next + jax.lax.ppermute(f_next, chip_axis, q)]
  transfers between devices with their start and end apart: 3 -> 5, of which waited for: 3 -> 5; matrix products, arithmetic and copies ran while one was open for 4% -> 4% of each run, Pallas kernels for 0% -> 0%
where the time goes in v1:
time: 866 us; the launch traced here: 854 us
  blocking collectives  307 us (35%)
  other arithmetic  169 us (20%)
  local copies, waits for them, and re-layouts  164 us (19%)
  matrix products  126 us (15%)
  waiting for transfers between devices  77.6 us (9%)
  starting transfers between devices  8.85 us (1%)
    all_to_all x2, blocking collectives, per_device(): lax.all_to_all(buffer.reshape(peer_count, capacity, layers, column_len),...  217 us
    scatter-add x2, other arithmetic, per_device(): jnp.zeros((columns, layers, column_len), jnp.float32).at[owned_column]  133 us
    scatter x2, local copies, waits for them, and re-layouts, per_device(): buffer = jnp.zeros((peer_count * capacity, layers, column_len), jnp.float...  112 us
    all_to_all x1, blocking collectives, per_device(): lax.all_to_all(outgoing.reshape(peer_count, capacity, column_len), ('bx',...  76.3 us
    dot_general x2, matrix products, per_device(): smeared = jnp.dot(quotient, blurring.T, precision=precise)  49.6 us
    dot_general x2, matrix products, per_device(): blurred = jnp.dot(forward, blurring, precision=precise)  48.7 us
    ppermute x4, waiting for transfers between devices, thing_raise(): f_next = f_next + jax.lax.ppermute(f_next, chip_axis, q)  40.3 us
    all_to_all x1, waiting for transfers between devices, per_device(): lax.all_to_all(outgoing.reshape(peer_count, capacity, column_len), ('bx',...  37.3 us
  transfers between devices with their start and end apart: 5, of which 5 were waited for; matrix products, arithmetic and copies ran while one was open for 4% of the time, Pallas kernels for 0%

profile of v1, /device:TPU:0, one launch (start us, length us, event | category | flops | bytes accessed | tf_op | source)
XLA Modules:
  0.0 853.9 jit_solution(4386617805516220012)
XLA Ops:
  1.8 2.3 reduce-window.6
  6.0 4.3 scatter_custom_fusion
  10.4 13.6 %all_to_all.29 = s32[8,1,192]{2,1,0:T(1,128)S(1)} all-to-all(s32[8,1,192]{2,1,0:T(1,128)S(1)} %all_to_all.18), channel_id=1, replica_groups=mesh['view'=4,'bx'=2,'by'=4] {'bx','by'}, dimensions={0} | all-to-all | bytes 12288 | tf_op jit(solution)/shard_map/all_to_all | solution.py:59
  24.3 5.0 gather_fusion
  29.2 5.1 all-to-all-start.1
  37.0 22.7 %fusion.58 = f32[512]{0:T(512)S(1)} fusion(f32[]{:T(128)} %bitcast.38, f32[]{:T(128)} %bitcast.37, f32[]{:T(128)} %bitcast.36, f32[]{:T(128)} %bitcast.35, f32[]{:T(128)} %bitcast.34, f32[]{:T(128)} %bitcast.33, f32[]{:T(128)} %bitcast.32, f32[]{:T(128)} %bitcast.31, f32[]{:T(128)} %bitcast.30, f32[]{:T(128)} %bitcast.29, f32[]{:T(128)} %bitcast.28, ...), kind=kLoop, calls=%fused_computation.73 | loop fusion | flops 24903168 | bytes 2172 | tf_op jit(solution)/shard_map/reduce_sum | solution.py:66
  59.7 5.7 fusion.4
  67.4 37.3 %all-to-all-done.1 = f32[8,192,512]{2,1,0:T(8,128)} async-done(((f32[8,192,512]{2,1,0:T(8,128)}), f32[8,192,512]{2,1,0:T(8,128)}, u32[]{:S(2)}, u32[]{:S(2)}) %all-to-all-start.1) | async-done | bytes 3145760 | tf_op jit(solution)/shard_map/all_to_all | solution.py:72
  104.7 5.9 gather_fusion.1
  112.3 7.2 fusion.14
  119.6 24.3 %convolution_divide_fusion.1 = f32[256,512]{1,0:T(8,128)S(1)} fusion(f32[256,512]{1,0:T(8,128)S(1)} %fusion.14, f32[1,256,512]{2,1,0:T(8,128)S(1)} %copy-done.5, f32[]{:T(128)} %bitcast.38, f32[]{:T(128)} %bitcast.37, f32[]{:T(128)} %bitcast.36, f32[]{:T(128)} %bitcast.35, f32[]{:T(128)} %bitcast.34, f32[]{:T(128)} %bitcast.33, f32[]{:T(128)} %bitcast.32, ...), kind=kOutput, calls=%fused_computation.25 | convolution fusion | flops 830078976 | bytes 1572988 | tf_op jit(solution)/shard_map/dot_general | solution.py:82
  143.9 24.8 %convolution_bitcast_fusion.1 = f32[256,512,1]{1,0,2:T(8,128)S(1)} fusion(f32[256,512]{1,0:T(8,128)S(1)} %convolution_divide_fusion.1, f32[]{:T(128)} %bitcast.38, f32[]{:T(128)} %bitcast.37, f32[]{:T(128)} %bitcast.36, f32[]{:T(128)} %bitcast.35, f32[]{:T(128)} %bitcast.34, f32[]{:T(128)} %bitcast.33, f32[]{:T(128)} %bitcast.32, f32[]{:T(128)} %bitcast.31, ...), kind=kOutput, calls=%fused_computation.29 | convolution fusion | flops 829947904 | bytes 1048700 | tf_op jit(solution)/shard_map/dot_general | solution.py:84
  168.7 3.7 fusion.6
  175.6 2.7 pad_maximum_fusion
  178.3 5.3 copy.45
  183.5 4.3 broadcast_in_dim.160
  187.9 104.3 %scatter_fusion = f32[1536,2,512]{2,1,0:T(2,128)} fusion(f32[1536,2,512]{2,1,0:T(2,128)} %broadcast_in_dim.160, s32[1024]{0:T(1024)S(1)} %bitcast.130, f32[1024,2,512]{2,1,0:T(2,128)} %copy.45), kind=kCustom, calls=%fused_computation.5 | custom fusion | bytes 12587008 | tf_op jit(solution)/shard_map/scatter | solution.py:100
  292.2 142.2 %all_to_all.30 = f32[8,192,2,512]{3,2,1,0:T(2,128)} all-to-all(f32[8,192,2,512]{3,2,1,0:T(2,128)} %bitcast.121), channel_id=1, replica_groups=mesh['view'=4,'bx'=2,'by'=4] {'bx','by'}, dimensions={0} | all-to-all | bytes 12582912 | tf_op jit(solution)/shard_map/all_to_all | solution.py:102
  434.6 122.5 %scatter_fusion.1 = f32[256,2,512]{2,1,0:T(2,128)S(1)} fusion(f32[256,2,512]{2,1,0:T(2,128)S(1)} %broadcast_in_dim.158, s32[1536]{0:T(1024)S(1)} %fusion.67, f32[1536,2,512]{2,1,0:T(2,128)} %bitcast.122), kind=kCustom, calls=%fused_computation.6 | custom fusion | flops 1572864 | bytes 18880512 | tf_op jit(solution)/shard_map/scatter-add | solution.py:111
  559.0 2.6 collective-permute-done
  564.7 23.5 %collective-permute-done.1 = f32[2,256,512]{2,0,1:T(2,128)S(1)} collective-permute-done((f32[2,256,512]{2,0,1:T(2,128)S(1)}, f32[2,256,512]{2,0,1:T(2,128)S(1)}, u32[]{:S(2)}, u32[]{:S(2)}) %collective-permute-start.1) | collective-permute-done | bytes 1048608 | tf_op jit(solution)/shard_map/ppermute | solution.py:17
  591.2 5.0 gather_fusion.2
  596.2 76.3 %all_to_all.31 = f32[8,192,512]{2,1,0:T(8,128)} all-to-all(f32[8,192,512]{2,1,0:T(8,128)} %bitcast.125), channel_id=1, replica_groups=mesh['view'=4,'bx'=2,'by'=4] {'bx','by'}, dimensions={0} | all-to-all | bytes 6291456 | tf_op jit(solution)/shard_map/all_to_all | solution.py:72
  672.5 5.9 gather_fusion.3
  680.1 7.2 fusion.19
  687.3 24.3 %convolution_divide_fusion = f32[256,512]{1,0:T(8,128)S(1)} fusion(f32[256,512]{1,0:T(8,128)S(1)} %fusion.19, f32[1,256,512]{2,1,0:T(8,128)S(1)} %copy-done.6, f32[]{:T(128)} %bitcast.38, f32[]{:T(128)} %bitcast.37, f32[]{:T(128)} %bitcast.36, f32[]{:T(128)} %bitcast.35, f32[]{:T(128)} %bitcast.34, f32[]{:T(128)} %bitcast.33, f32[]{:T(128)} %bitcast.32, ...), kind=kOutput, calls=%fused_computation.24 | convolution fusion | flops 830078976 | bytes 1572988 | tf_op jit(solution)/shard_map/dot_general | solution.py:82
  711.7 24.8 %convolution_bitcast_fusion = f32[256,512,1]{1,0,2:T(8,128)S(1)} fusion(f32[256,512]{1,0:T(8,128)S(1)} %convolution_divide_fusion, f32[]{:T(128)} %bitcast.38, f32[]{:T(128)} %bitcast.37, f32[]{:T(128)} %bitcast.36, f32[]{:T(128)} %bitcast.35, f32[]{:T(128)} %bitcast.34, f32[]{:T(128)} %bitcast.33, f32[]{:T(128)} %bitcast.32, f32[]{:T(128)} %bitcast.31, ...), kind=kOutput, calls=%fused_computation.28 | convolution fusion | flops 829947904 | bytes 1048700 | tf_op jit(solution)/shard_map/dot_general | solution.py:84
  736.5 3.7 fusion
  743.3 7.3 scatter_custom_fusion.3
  750.6 75.2 %all_to_all.32 = f32[8,192,1,512]{3,1,2,0:T(8,128)} all-to-all(f32[8,192,1,512]{3,1,2,0:T(8,128)} %bitcast.123), channel_id=1, replica_groups=mesh['view'=4,'bx'=2,'by'=4] {'bx','by'}, dimensions={0} | all-to-all | bytes 6291456 | tf_op jit(solution)/shard_map/all_to_all | solution.py:102
  825.7 10.8 %scatter_custom_fusion.4 = f32[256,512]{1,0:T(8,128)S(1)} fusion(s32[1536]{0:T(1024)S(1)} %fusion.67, f32[1536,512]{1,0:T(8,128)} %bitcast.126, f32[]{:T(128)} %constant.37.clone.1), kind=kCustom, calls=%fused_computation.74 | custom fusion | flops 786432 | bytes 524800 | tf_op jit(solution)/shard_map/scatter-add | solution.py:111
  840.4 12.3 %collective-permute-done.3 = f32[1,256,512]{2,1,0:T(8,128)S(1)} collective-permute-done((f32[1,256,512]{2,1,0:T(8,128)S(1)}, f32[1,256,512]{2,1,0:T(8,128)S(1)}, u32[]{:S(2)}, u32[]{:S(2)}) %collective-permute-start.3) | collective-permute-done | bytes 524320 | tf_op jit(solution)/shard_map/ppermute | solution.py:17
  (69 shorter events, 31.3 us)
Async XLA Ops:
  0.0 24.2 %copy-start = (f32[256,512]{1,0:T(8,128)S(1)}, f32[256,512]{1,0:T(8,128)}, u32[]{:S(2)}) copy-start(f32[256,512]{1,0:T(8,128)} %param.6) | copy-start | bytes 1572868
  29.2 5.1 copy-start.7
  29.2 75.5 %all-to-all-start.1 = ((f32[8,192,512]{2,1,0:T(8,128)}), f32[8,192,512]{2,1,0:T(8,128)}, u32[]{:S(2)}, u32[]{:S(2)}) async-start(f32[8,192,512]{2,1,0:T(8,128)} %bitcast.124), calls=%async_computation.1 | async-start | bytes 6291456 | tf_op jit(solution)/shard_map/all_to_all | solution.py:72
  112.3 7.2 copy-start.5
  143.9 24.8 %copy-start.1 = (f32[1,4,512,512]{3,2,1,0:T(8,128)S(1)}, f32[1,4,512,512]{3,2,1,0:T(8,128)}, u32[]{:S(2)}) copy-start(f32[1,4,512,512]{3,2,1,0:T(8,128)} %param.8) | copy-start | bytes 12582916
  558.9 2.7 collective-permute-start
  562.8 25.3 %collective-permute-start.1 = (f32[2,256,512]{2,0,1:T(2,128)S(1)}, f32[2,256,512]{2,0,1:T(2,128)S(1)}, u32[]{:S(2)}, u32[]{:S(2)}) collective-permute-start(f32[2,256,512]{2,0,1:T(2,128)S(1)} %fusion.198), channel_id=1, source_target_pairs={{0,16},{8,24},{16,0},{24,8},{1,17},{9,25},{17,1},{25,9},{2,18},{10... | collective-permute-start | bytes 3145736 | tf_op jit(solution)/shard_map/ppermute | solution.py:17
  590.2 0.8 copy-start.3
  680.1 7.2 copy-start.6
  711.6 24.8 %copy-start.2 = (f32[1,4,512,512]{3,2,1,0:T(8,128)S(1)}, f32[1,4,512,512]{3,2,1,0:T(8,128)}, u32[]{:S(2)}) copy-start(f32[1,4,512,512]{3,2,1,0:T(8,128)} %param.8) | copy-start | bytes 12582916
  750.6 102.1 %copy-start.4 = (f32[1,256,512]{2,0,1:T(1,128)S(1)}, f32[1,256,512]{2,0,1:T(1,128)}, u32[]{:S(2)}) copy-start(f32[1,256,512]{2,0,1:T(1,128)} %copy-done.3) | copy-start | bytes 1572868
  836.6 2.0 collective-permute-start.2
  838.6 14.0 %collective-permute-start.3 = (f32[1,256,512]{2,1,0:T(8,128)S(1)}, f32[1,256,512]{2,1,0:T(8,128)S(1)}, u32[]{:S(2)}, u32[]{:S(2)}) collective-permute-start(f32[1,256,512]{2,1,0:T(8,128)S(1)} %bitcast_add_fusion), channel_id=1, source_target_pairs={{0,16},{8,24},{16,0},{24,8},{1,17},{9,25},{17,1},{25,9},{2,18},{10... | collective-permute-start | bytes 1572872 | tf_op jit(solution)/shard_map/ppermute | solution.py:17
